TPU v7x, 256 devices: a whole 4x4x8 slice. The times are simulated.
256 devices in a mesh: dp: 2 (over core), seq: 8 (over z), expert: 16 (over y, x).
Axes of the slice: x: 4, y: 4, z: 8, core: 2. Of those that a mesh axis runs over, the one named last changes fastest.
Arguments:
- tokens: bfloat16 [16384, 2048], P(('dp', 'seq')), may hold values from -6 to 6
- phi: bfloat16 [2048, 32], P(None, 'expert'), may hold values from -40 to 40
- w_in: bfloat16 [32, 2048, 8192], P('expert', None, ('dp', 'seq')), may hold values from -1 to 1
- w_out: bfloat16 [32, 8192, 2048], P('expert', ('dp', 'seq')), may hold values from -0.25 to 0.25
Outputs:
- mixed: bfloat16 [16384, 2048], P(('dp', 'seq', 'expert'))
All inputs are finite; a program needn't handle non-finite values.
Results may differ from a plain program's by a relative error of at most 0.0068.
Values may be sent and summed in bfloat16 or wider, within the bound.
A program may use at most 64 MiB of HBM per device.

v0:
```python
import jax
import jax.numpy as jnp
from jax import lax
from jax.sharding import PartitionSpec as P


def on_device(tokens, phi, w_in, w_out):
    logits = lax.dot_general(
        phi, tokens, (((0,), (1,)), ((), ())), preferred_element_type=jnp.float32
    )
    slot_max = lax.pmax(jnp.max(logits, axis=1), "seq")
    spread = jnp.exp(logits - slot_max[:, None])
    numerator = jnp.dot(spread.astype(jnp.bfloat16), tokens, preferred_element_type=jnp.float32)
    denominator = jnp.sum(spread, axis=1)
    numer_seq, denom_seq = lax.psum((numerator, denominator), "seq")
    own_slots = (numer_seq / denom_seq[:, None]).astype(jnp.bfloat16)
    slot_in = lax.all_gather(own_slots[None], "dp", axis=0, tiled=True)
    hidden = jax.nn.gelu(
        jnp.einsum("ced,edf->cef", slot_in, w_in, preferred_element_type=jnp.float32),
        approximate=True,
    ).astype(jnp.bfloat16)
    partial_value = jnp.einsum("cef,efd->ced", hidden, w_out, preferred_element_type=jnp.float32)
    totals = lax.psum(partial_value, ("dp", "seq"))
    summed = lax.dynamic_index_in_dim(totals, lax.axis_index("dp"), 0, keepdims=False)
    slot_out = summed.astype(jnp.bfloat16)
    row_max = lax.pmax(jnp.max(logits, axis=0), "expert")
    combine_weights = jnp.exp(logits - row_max[None, :])
    local_numer = lax.dot_general(
        combine_weights.astype(jnp.bfloat16),
        slot_out,
        (((0,), (0,)), ((), ())),
        preferred_element_type=jnp.float32,
    )
    mixed_numer, mixed_denom = (
        lax.psum_scatter(local_numer, "expert", scatter_dimension=0, tiled=True),
        lax.psum_scatter(
            jnp.sum(combine_weights, axis=0), "expert", scatter_dimension=0, tiled=True
        ),
    )
    return (mixed_numer / mixed_denom[:, None]).astype(jnp.bfloat16)


def solution(mesh):
    placed = (
        P(("dp", "seq"), None),
        P(None, "expert"),
        P("expert", None, ("dp", "seq")),
        P("expert", ("dp", "seq"), None),
    )
    return jax.shard_map(
        on_device,
        mesh=mesh,
        in_specs=placed,
        out_specs=P(("dp", "seq", "expert"), None),
        check_vma=False,
    )
```

profile of v0, /device:TPU:2, one launch (start us, length us, event | category | flops | bytes accessed | tf_op | source)
XLA Modules:
  0.0 258.3 jit_solution(14364468299653725748)
XLA Ops:
  6.5 0.0 copy-start
  6.5 0.0 reduce-scatter.2.cloned.1.call-start
  6.5 0.7 copy-done
  7.2 3.5 %fusion.35 = (f32[1024]{0:T(1024)S(1)}, f32[2]{0:T(128)S(1)}, f32[2,1024]{1,0:T(2,128)S(1)}) fusion(bf16[2048,2]{0,1:T(2,128)(2,1)S(1)} %copy-done, bf16[1024,2048]{1,0:T(8,128)(2,1)} %param.4), kind=kOutput, calls=%fused_computation.35 | convolution fusion | flops 8391678 | bytes 4214792 | tf_op jit(solution)/shard_map/dot_general | solution.py:8
  10.7 37.7 %pmax.14 = f32[1024]{0:T(1024)S(1)} all-reduce(f32[1024]{0:T(1024)S(1)} %get-tuple-element.7), channel_id=1, replica_groups=mesh['dp'=2,'seq'=8,'expert'=16] {'expert'}, use_global_device_ids=true, to_apply=%region_1.0 | all-reduce | flops 1024 | bytes 8192 | tf_op jit(solution)/shard_map/pmax | solution.py:26
  48.4 19.0 %pmax.15 = f32[2]{0:T(128)S(1)} all-reduce(f32[2]{0:T(128)S(1)} %get-tuple-element.8), channel_id=1, replica_groups=mesh['dp'=2,'seq'=8,'expert'=16] {'seq'}, use_global_device_ids=true, to_apply=%region_3.0 | all-reduce | flops 2 | bytes 16 | tf_op jit(solution)/shard_map/pmax | solution.py:11
  67.4 2.9 %fusion.23 = f32[2,2048]{1,0:T(2,128)S(1)} fusion(bf16[1024,2048]{1,0:T(8,128)(2,1)} %param.4, f32[2,1024]{1,0:T(2,128)S(1)} %get-tuple-element.11, f32[2]{0:T(128)S(1)} %pmax.15), kind=kOutput, calls=%fused_computation.25 | convolution fusion | flops 8392704 | bytes 4218888 | tf_op jit(solution)/shard_map/dot_general | solution.py:13
  70.3 0.2 fusion.19
  70.5 27.1 %all-reduce.1 = (f32[2,2048]{1,0:T(2,128)S(1)}, f32[2]{0:T(128)S(1)}) all-reduce(f32[2,2048]{1,0:T(2,128)S(1)} %fusion.23, f32[2]{0:T(128)S(1)} %get-tuple-element.6), channel_id=1, replica_groups=mesh['dp'=2,'seq'=8,'expert'=16] {'seq'}, use_global_device_ids=true, to_apply=%region_4.0 | all-reduce | flops 4098 | bytes 32784 | tf_op jit(solution)/shard_map/psum | solution.py:15
  97.6 0.1 fusion.18
  97.6 1.8 all-gather.1
  99.4 4.7 %convolution_bitcast_fusion = f32[2,2,2048]{2,0,1:T(2,128)S(1)} fusion(bf16[2,512,2048]{2,1,0:T(8,128)(2,1)} %param.7, bf16[2,2048,512]{2,1,0:T(8,128)(2,1)} %param.6, bf16[2,2,2048]{2,1,0:T(2,128)(2,1)S(1)} %all-gather.1), kind=kOutput, calls=%fused_computation | convolution fusion | flops 16795648 | bytes 8437760 | tf_op jit(solution)/shard_map/cef,efd->ced/dot_general | solution.py:22
  104.1 50.2 %psum.23 = bf16[2,2,2048]{2,0,1:T(2,128)(2,1)S(1)} all-reduce(f32[2,2,2048]{2,0,1:T(2,128)S(1)} %convolution_bitcast_fusion), channel_id=1, replica_groups=mesh['dp'=2,'seq'=8,'expert'=16] {'dp','seq'}, use_global_device_ids=true, to_apply=%region_7.8 | all-reduce | flops 8192 | bytes 49152 | tf_op jit(solution)/shard_map/psum | solution.py:23
  154.3 4.5 %fusion.15 = f32[1024,2048]{1,0:T(8,128)} fusion(bf16[1,2,2048]{2,0,1:T(2,128)(2,1)S(1)} %dynamic-slice_convert_fusion, f32[2,1024]{1,0:T(2,128)S(1)} %get-tuple-element.11, f32[1024]{0:T(1024)S(1)} %pmax.14), kind=kOutput, calls=%fused_computation.15 | convolution fusion | flops 8392704 | bytes 8409088 | tf_op jit(solution)/shard_map/dot_general | solution.py:28
  158.9 0.0 copy-start.1
  158.9 0.0 reduce-scatter.2.cloned.1.call-update
  158.9 0.6 copy-done.1
  159.5 0.6 dynamic-slice
  160.8 40.2 %all-reduce = f32[1024]{0:T(1024)S(1)} all-reduce(f32[1024]{0:T(1024)S(1)} %get-tuple-element.5), channel_id=4, replica_groups=mesh['dp'=2,'seq'=8,'expert'=16] {'expert'}, use_global_device_ids=true, to_apply=%region_10.11.clone | all-reduce | flops 1024 | bytes 8192
  201.0 0.1 dynamic-slice.1
  201.1 48.5 %reduce-scatter.2.cloned.1.call-done = f32[64,2048]{1,0:T(8,128)} async-done(((f32[1024,2048]{1,0:T(8,128)}), f32[64,2048]{1,0:T(8,128)}) %reduce-scatter.2.cloned.1.call-update) | async-done | bytes 524304 | tf_op jit(solution)/shard_map/reduce_scatter | solution.py:35
  249.6 1.8 divide_convert_fusion
  (1 shorter events, 0.0 us)
Async XLA Ops:
  6.5 0.7 copy-start
  6.5 243.0 %reduce-scatter.2.cloned.1.call-start = ((), (), s32[]{:S(2)}) async-start(), calls=%async_computation.1 | async-start | bytes 8912896 | tf_op jit(solution)/shard_map/reduce_scatter | solution.py:35
  158.9 0.7 copy-start.1
Sparse Core Ops, SparseCore 0:
  159.0 90.5 reduce-scatter.1
where the time goes:
time: 259 us; the launch traced here: 258 us
  blocking collectives  176 us (68%)
  waiting for transfers between devices  48.5 us (19%)
  matrix products  15.6 us (6%)
  between operations  14.1 us (5%)
    psum x1, blocking collectives, on_device(): totals = lax.psum(partial_value, ('dp', 'seq'))  50.2 us
    reduce_scatter x1, waiting for transfers between devices, on_device(): lax.psum_scatter(local_numer, 'expert', scatter_dimension=0, tiled=True)  48.5 us
    unnamed x1, blocking collectives  40.2 us
    pmax x1, blocking collectives, on_device(): row_max = lax.pmax(jnp.max(logits, axis=0), 'expert')  37.7 us
    psum x1, blocking collectives, on_device(): numer_seq, denom_seq = lax.psum((numerator, denominator), 'seq')  27.1 us
    pmax x1, blocking collectives, on_device(): slot_max = lax.pmax(jnp.max(logits, axis=1), 'seq')  19 us
  transfers between devices with their start and end apart: 1, of which 1 were waited for; matrix products, arithmetic and copies ran while one was open for 0% of the time, Pallas kernels for 0%

commit v1 on v0

--- a/solution.py
+++ b/solution.py
@@ -20,7 +20,7 @@
         approximate=True,
     ).astype(jnp.bfloat16)
     partial_value = jnp.einsum("cef,efd->ced", hidden, w_out, preferred_element_type=jnp.float32)
-    totals = lax.psum(partial_value, ("dp", "seq"))
+    totals = lax.psum(lax.psum(partial_value, "seq"), "dp")
     summed = lax.dynamic_index_in_dim(totals, lax.axis_index("dp"), 0, keepdims=False)
     slot_out = summed.astype(jnp.bfloat16)
     row_max = lax.pmax(jnp.max(logits, axis=0), "expert")

time: 259 us -> 236 us (0.911)
  blocking collectives: 176 us -> 157 us
  waiting for transfers between devices: 48.5 us -> 45.5 us
    psum x1 -> x2, blocking collectives: 50.2 us -> 30.9 us  [on_device(): totals = lax.psum(lax.psum(partial_value, 'seq'), 'dp')]
    reduce_scatter x1, waiting for transfers between devices: 48.5 us -> 45.5 us  [on_device(): lax.psum_scatter(local_numer, 'expert', scatter_dimension=0, tiled=True)]
where the time goes in v1:
time: 236 us
  blocking collectives  157 us (67%)
  waiting for transfers between devices  45.5 us (19%)
  matrix products  15.6 us (7%)
  between operations  14.1 us (6%)
    reduce_scatter x1, waiting for transfers between devices, on_device(): lax.psum_scatter(local_numer, 'expert', scatter_dimension=0, tiled=True)  45.5 us
    unnamed x1, blocking collectives  40.2 us
    pmax x1, blocking collectives, on_device(): row_max = lax.pmax(jnp.max(logits, axis=0), 'expert')  37.7 us
    psum x2, blocking collectives, on_device(): totals = lax.psum(lax.psum(partial_value, 'seq'), 'dp')  30.9 us
    psum x1, blocking collectives, on_device(): numer_seq, denom_seq = lax.psum((numerator, denominator), 'seq')  27.1 us
    pmax x1, blocking collectives, on_device(): slot_max = lax.pmax(jnp.max(logits, axis=1), 'seq')  19 us
  transfers between devices with their start and end apart: 1, of which 1 were waited for; matrix products, arithmetic and copies ran while one was open for 0% of the time, Pallas kernels for 0%

profile of v1, /device:TPU:2, one launch (start us, length us, event | category | flops | bytes accessed | tf_op | source)
XLA Modules:
  0.0 236.0 jit_solution(6344803138465717594)
XLA Ops:
  6.5 0.0 copy-start
  6.5 0.0 reduce-scatter.2.cloned.1.call-start
  6.5 0.7 copy-done
  7.2 3.5 %fusion.35 = (f32[1024]{0:T(1024)S(1)}, f32[2]{0:T(128)S(1)}, f32[2,1024]{1,0:T(2,128)S(1)}) fusion(bf16[2048,2]{0,1:T(2,128)(2,1)S(1)} %copy-done, bf16[1024,2048]{1,0:T(8,128)(2,1)} %param.4), kind=kOutput, calls=%fused_computation.35 | convolution fusion | flops 8391678 | bytes 4214792 | tf_op jit(solution)/shard_map/dot_general | solution.py:8
  10.7 37.7 %pmax.14 = f32[1024]{0:T(1024)S(1)} all-reduce(f32[1024]{0:T(1024)S(1)} %get-tuple-element.7), channel_id=1, replica_groups=mesh['dp'=2,'seq'=8,'expert'=16] {'expert'}, use_global_device_ids=true, to_apply=%region_1.0 | all-reduce | flops 1024 | bytes 8192 | tf_op jit(solution)/shard_map/pmax | solution.py:26
  48.4 19.0 %pmax.15 = f32[2]{0:T(128)S(1)} all-reduce(f32[2]{0:T(128)S(1)} %get-tuple-element.8), channel_id=1, replica_groups=mesh['dp'=2,'seq'=8,'expert'=16] {'seq'}, use_global_device_ids=true, to_apply=%region_3.0 | all-reduce | flops 2 | bytes 16 | tf_op jit(solution)/shard_map/pmax | solution.py:11
  67.4 2.9 %fusion.23 = f32[2,2048]{1,0:T(2,128)S(1)} fusion(bf16[1024,2048]{1,0:T(8,128)(2,1)} %param.4, f32[2,1024]{1,0:T(2,128)S(1)} %get-tuple-element.11, f32[2]{0:T(128)S(1)} %pmax.15), kind=kOutput, calls=%fused_computation.25 | convolution fusion | flops 8392704 | bytes 4218888 | tf_op jit(solution)/shard_map/dot_general | solution.py:13
  70.3 0.2 fusion.19
  70.5 27.1 %all-reduce.1 = (f32[2,2048]{1,0:T(2,128)S(1)}, f32[2]{0:T(128)S(1)}) all-reduce(f32[2,2048]{1,0:T(2,128)S(1)} %fusion.23, f32[2]{0:T(128)S(1)} %get-tuple-element.6), channel_id=1, replica_groups=mesh['dp'=2,'seq'=8,'expert'=16] {'seq'}, use_global_device_ids=true, to_apply=%region_4.0 | all-reduce | flops 4098 | bytes 32784 | tf_op jit(solution)/shard_map/psum | solution.py:15
  97.6 0.1 fusion.18
  97.6 1.8 all-gather.1
  99.4 4.7 %convolution_bitcast_fusion = f32[2,2,2048]{2,0,1:T(2,128)S(1)} fusion(bf16[2,512,2048]{2,1,0:T(8,128)(2,1)} %param.7, bf16[2,2048,512]{2,1,0:T(8,128)(2,1)} %param.6, bf16[2,2,2048]{2,1,0:T(2,128)(2,1)S(1)} %all-gather.1), kind=kOutput, calls=%fused_computation | convolution fusion | flops 16795648 | bytes 8437760 | tf_op jit(solution)/shard_map/cef,efd->ced/dot_general | solution.py:22
  104.1 27.6 %psum.30 = f32[2,2,2048]{2,0,1:T(2,128)S(1)} all-reduce(f32[2,2,2048]{2,0,1:T(2,128)S(1)} %convolution_bitcast_fusion), channel_id=1, replica_groups=mesh['dp'=2,'seq'=8,'expert'=16] {'seq'}, use_global_device_ids=true, to_apply=%region_7.8 | all-reduce | flops 8192 | bytes 65536 | tf_op jit(solution)/shard_map/psum | solution.py:23
  131.6 3.4 %psum.31 = bf16[2,2,2048]{2,0,1:T(2,128)(2,1)S(1)} all-reduce(f32[2,2,2048]{2,0,1:T(2,128)S(1)} %psum.30), channel_id=1, replica_groups=mesh['dp'=2,'seq'=8,'expert'=16] {'dp'}, use_global_device_ids=true, to_apply=%region_8.9 | all-reduce | flops 8192 | bytes 49152 | tf_op jit(solution)/shard_map/psum | solution.py:23
  135.1 4.5 %fusion.15 = f32[1024,2048]{1,0:T(8,128)} fusion(bf16[1,2,2048]{2,0,1:T(2,128)(2,1)S(1)} %dynamic-slice_convert_fusion, f32[2,1024]{1,0:T(2,128)S(1)} %get-tuple-element.11, f32[1024]{0:T(1024)S(1)} %pmax.14), kind=kOutput, calls=%fused_computation.15 | convolution fusion | flops 8392704 | bytes 8409088 | tf_op jit(solution)/shard_map/dot_general | solution.py:28
  139.6 0.0 copy-start.1
  139.6 0.0 reduce-scatter.2.cloned.1.call-update
  139.6 0.6 copy-done.1
  140.3 0.6 dynamic-slice
  141.5 40.2 %all-reduce = f32[1024]{0:T(1024)S(1)} all-reduce(f32[1024]{0:T(1024)S(1)} %get-tuple-element.5), channel_id=4, replica_groups=mesh['dp'=2,'seq'=8,'expert'=16] {'expert'}, use_global_device_ids=true, to_apply=%region_11.12.clone | all-reduce | flops 1024 | bytes 8192
  181.7 0.1 dynamic-slice.1
  181.8 45.5 %reduce-scatter.2.cloned.1.call-done = f32[64,2048]{1,0:T(8,128)} async-done(((f32[1024,2048]{1,0:T(8,128)}), f32[64,2048]{1,0:T(8,128)}) %reduce-scatter.2.cloned.1.call-update) | async-done | bytes 524304 | tf_op jit(solution)/shard_map/reduce_scatter | solution.py:35
  227.3 1.8 divide_convert_fusion
  (1 shorter events, 0.0 us)
Async XLA Ops:
  6.5 0.7 copy-start
  6.5 220.8 %reduce-scatter.2.cloned.1.call-start = ((), (), s32[]{:S(2)}) async-start(), calls=%async_computation.1 | async-start | bytes 8912896 | tf_op jit(solution)/shard_map/reduce_scatter | solution.py:35
  139.6 0.7 copy-start.1
Sparse Core Ops, SparseCore 0:
  139.8 87.5 reduce-scatter.1
